TPU v7x, 32 devices: a whole 2x2x4 slice. The times are simulated.
32 devices in a mesh: space: 4 (over y, core), vel: 8 (over z, x).
Axes of the slice: x: 2, y: 2, z: 4, core: 2. Of those that a mesh axis runs over, the one named last changes fastest.
Arguments:
- distribution: float32 [64, 48, 2304], P('space', 'vel'), may hold values from 0 to 2
- collision_rate: float32 [64], P('space'), may hold values from 0.1 to 1
- face_flags: int32 [64], replicated, may hold values 0 or 1
Outputs:
- updated: float32 [64, 48, 2304], P('space', 'vel')
All inputs are finite; a program needn't handle non-finite values.
Results may differ from a plain program's by a relative error of at most 0.0001.
Values sent between devices are 32-bit elements; how exact they have to be, the bound alone decides.
A program may use at most 64 MiB of HBM per device.

v0:
```python
import math
import jax
import jax.numpy as jnp
from jax import lax
from jax.sharding import PartitionSpec as P

NV = 48
LENGTH = 8.0
RADIUS = 6.0
COURANT = 0.9
GOLDEN = (1.0 + math.sqrt(5.0)) / 2.0
DIRECTIONS = (
    (0.0, 1.0, GOLDEN),
    (0.0, -1.0, GOLDEN),
    (1.0, GOLDEN, 0.0),
    (-1.0, GOLDEN, 0.0),
    (GOLDEN, 0.0, 1.0),
    (-GOLDEN, 0.0, 1.0),
)
HIGHEST_MODE = lax.Precision.HIGHEST


def padded_2(cells, sides, width):
    for axis, dim in sides:
        count = lax.axis_size(axis)
        ends = count - 1
        head = lax.slice_in_dim(cells, 0, width, axis=dim)
        tail = lax.slice_in_dim(cells, cells.shape[dim] - width, cells.shape[dim], axis=dim)
        cells = jnp.concatenate(
            [
                lax.ppermute(tail, axis, [(i, (i + 1) % count) for i in range(ends)]),
                cells,
                lax.ppermute(head, axis, [((i + 1) % count, i) for i in range(ends)]),
            ],
            axis=dim,
        )
    return cells


def kernel_tables(points):
    index = jnp.arange(points, dtype=jnp.int32)
    wrapped = jnp.where(
        index < points // 2, index, jnp.where(index == points // 2, 0, index - points)
    )
    signed = wrapped.astype(jnp.float32) * (math.pi / LENGTH)
    wave_x = signed[:, None, None]
    wave_y = signed[None, :, None]
    wave_z = signed[None, None, :]
    square = wave_x * wave_x + wave_y * wave_y + wave_z * wave_z
    scale = math.sqrt(1.0 + GOLDEN * GOLDEN)
    gain_tables = []
    loss_tables = []
    for direction in DIRECTIONS:
        parallel = (wave_x * direction[0] + wave_y * direction[1] + wave_z * direction[2]) / scale
        across = jnp.sqrt(jnp.maximum(square - parallel * parallel, 0.0))
        gain_tables.append(jnp.cos(0.5 * RADIUS * parallel))
        loss_tables.append(jnp.sinc(RADIUS * across / (2.0 * math.pi)))
    loss_total = sum(loss_tables) / 6.0
    return (gain_tables, loss_tables, loss_total)


def dft_tables(points):
    index = jnp.arange(points, dtype=jnp.int32)
    product = index[:, None] * index[None, :] % points
    angle = product.astype(jnp.float32) * (2.0 * math.pi / points)
    cosine = jnp.cos(angle)
    sine = jnp.sin(angle)
    first_table = jnp.stack([cosine, -sine], axis=1)
    forward_table = jnp.stack(
        [jnp.stack([cosine, -sine], axis=1), jnp.stack([sine, cosine], axis=1)], axis=1
    )
    inverse_table = jnp.stack(
        [jnp.stack([cosine, sine], axis=1), jnp.stack([-sine, cosine], axis=1)], axis=1
    )
    return (first_table, forward_table, inverse_table)


def apply_table(tensor, table, dims):
    return lax.dot_general(
        tensor,
        table,
        ((dims, tuple(range(len(dims)))), ((), ())),
        precision=HIGHEST_MODE,
        preferred_element_type=jnp.float32,
    )


def forward_cube(cube, tables):
    first_table, forward_table, inverse_table = tables
    section_one = apply_table(cube, first_table, (1,))
    section_two = apply_table(section_one, forward_table, (1, 2))
    return apply_table(section_two, forward_table, (0, 2))


def inverse_pair(spectrum, tables):
    first_table, forward_table, inverse_table = tables
    points = spectrum.shape[0]
    section_one = apply_table(spectrum, inverse_table, (3, 2))
    section_two = apply_table(section_one, inverse_table, (0, 2))
    section_three = apply_table(section_two, inverse_table, (0, 2))
    section_three = section_three * (1.0 / float(points**3))
    return (section_three[:, :, 0, :], section_three[:, :, 1, :])


def packed(spectrum, first_factor, second_factor):
    real_part = spectrum[:, :, 0, :]
    imag_part = spectrum[:, :, 1, :]
    first_factor = jnp.asarray(first_factor, jnp.float32)
    first_factor = first_factor[:, :, :] if first_factor.ndim == 3 else first_factor
    joined_real = first_factor * real_part - second_factor * imag_part
    joined_imag = first_factor * imag_part + second_factor * real_part
    return jnp.stack([joined_real, joined_imag], axis=2)


def collide(spectrum, kernels, tables):
    gain_tables, loss_tables, loss_total = kernels
    products = []
    for gain_table, loss_table in zip(gain_tables, loss_tables):
        first_part, second_part = inverse_pair(packed(spectrum, gain_table, loss_table), tables)
        products.append(first_part * second_part)
    gain_total = sum(products) / 6.0
    cube, loss_field = inverse_pair(packed(spectrum, 1.0, loss_total), tables)
    return gain_total - cube * loss_field


def body(distribution, collision_rate, face_flags):
    cell_count, planes_dev, width = distribution.shape
    points = NV
    tables = dft_tables(points)
    kernels = kernel_tables(points)

    def from_cell(one_cell):
        cube = one_cell.reshape(points, points, points)
        spectrum = forward_cube(cube, tables)
        return collide(spectrum, kernels, tables).reshape(points, width)

    regrouped = lax.all_to_all(distribution, "vel", split_axis=0, concat_axis=1, tiled=True)
    cell_terms = lax.map(from_cell, regrouped)
    collision_term = lax.all_to_all(cell_terms, "vel", split_axis=1, concat_axis=0, tiled=True)
    offset = lax.axis_index("space") * cell_count
    padded = padded_2(distribution, (("space", 0),), 1)
    mirror = distribution.reshape(cell_count, planes_dev, points, points)[:, :, ::-1, :].reshape(
        cell_count, planes_dev, width
    )
    wall_flags = jnp.concatenate([face_flags, jnp.ones((1,), jnp.int32)])
    nearby_walls = lax.dynamic_slice_in_dim(wall_flags, offset, cell_count + 1)
    lower_wall = (nearby_walls[:-1] == 1)[:, None, None]
    upper_wall = (nearby_walls[1:] == 1)[:, None, None]
    at_start = (offset + jnp.arange(cell_count, dtype=jnp.int32) == 0)[:, None, None]
    lower_side = jnp.where(lower_wall, mirror, jnp.where(at_start, distribution, padded[:-2]))
    upper_side = jnp.where(upper_wall, mirror, padded[2:])
    column = (jnp.arange(width, dtype=jnp.int32) // points).astype(jnp.float32)
    centre = (points - 1) / 2.0
    speed = COURANT * (column - centre) / centre
    upwind_flux = jnp.where(
        speed > 0, speed * (distribution - lower_side), speed * (upper_side - distribution)
    )
    return distribution - upwind_flux + collision_rate[:, None, None] * collision_term


def solution(mesh):
    return jax.shard_map(
        body,
        mesh=mesh,
        in_specs=(P("space", "vel", None), P("space"), P()),
        out_specs=P("space", "vel", None),
        check_vma=False,
    )
```

profile of v0, /device:TPU:0, one launch (start us, length us, event | category | flops | bytes accessed | tf_op | source)
XLA Modules:
  0.0 418.8 jit_solution(5220611589307567298)
XLA Ops:
  2.8 7.3 %all-to-all-start = ((f32[16,6,2304]{2,1,0:T(8,128)}), f32[16,6,2304]{2,1,0:T(8,128)S(1)}, u32[]{:S(2)}, u32[]{:S(2)}) async-start(f32[16,6,2304]{2,1,0:T(8,128)} %copy.77), calls=%async_computation | async-start | bytes 2359296 | tf_op jit(solution)/shard_map/all_to_all | solution.py:137
  10.6 13.5 %add_multiply_fusion = (f32[48,48,48]{2,1,0:T(8,128)}, f32[48,48,48]{2,1,0:T(8,128)}, f32[48,48,48]{2,1,0:T(8,128)}, f32[48,48,48]{2,1,0:T(8,128)}, f32[48,48,48...) fusion(f32[48]{0:T(128)S(1)} %get-tuple-element.737, f32[48,48]{1,0:T(8,128)S(1)} %get-tuple-element.739, ...), kind=kLoop, calls=%fused_computation.329 | loop fusion | flops 26652672 | bytes 3161856 | tf_op jit(solution)/shard_map/div | solution.py:58
  24.2 14.4 %all-to-all-done = f32[16,6,2304]{2,1,0:T(8,128)S(1)} async-done(((f32[16,6,2304]{2,1,0:T(8,128)}), f32[16,6,2304]{2,1,0:T(8,128)S(1)}, u32[]{:S(2)}, u32[]{:S(2)}) %all-to-all-start) | async-done | bytes 884768 | tf_op jit(solution)/shard_map/all_to_all | solution.py:137
  39.3 347.2 %while.13 = (s32[]{:T(128)}, f32[2,48,2304]{2,0,1:T(2,128)}, f32[2,48,2304]{2,0,1:T(2,128)S(1)}, f32[48,2,48]{2,0,1:T(8,128)S(1)}, f32[48,2,2,48]{3,0,1,2:T(8,12...) while((s32[]{:T(128)}, f32[2,48,2304]{2,0,1:T(2,128)}, ...), condition=%wide.region_1.3_spmd.clone.clone.clone, body=%wide.region_0.2_spmd.clone.clone.clone.sunk | while | flops 5998288896 | bytes 128030208 | solution.py:138
  49.0 6.0 %fusion.365 = f32[48,48,2,48,1]{0,3,4,2,1:T(8,128)S(1)} fusion(f32[48,48,2,48,1]{1,0,2,4,3:T(8,128)} %copy.170, f32[48,2,2,48]{3,0,1,2:T(8,128)S(1)} %get-tuple-element.770), kind=kOutput, calls=%fused_computation.156.clone.1 | convolution fusion | flops 254803968 | bytes 1806336 | tf_op jit(solution)/shard_map/while/body/eval_jaxpr/dot_general | solution.py:79
  57.1 10.0 %fusion.367 = (f32[48,48,1,48]{3,1,2,0:T(8,128)}, f32[48,48,1,48]{3,1,2,0:T(8,128)}, f32[48,48,1,48]{3,1,2,0:T(8,128)S(1)}, f32[48,48,1,48]{3,1,2,0:T(8,128)S(1)...) fusion(f32[48,48,48]{2,1,0:T(8,128)S(1)} %copy-done.16, f32[48]{0:T(128)S(1)} %get-tuple-element.779, ...), kind=kLoop, calls=%fused_computation.117.clone.1 | loop fusion | flops 2211840 | bytes 4884672 | tf_op jit(solution)/shard_map/while/body/eval_jaxpr/sub | solution.py:110
  74.5 6.0 %fusion.381 = f32[48,48,2,48,1]{0,3,4,2,1:T(8,128)S(1)} fusion(f32[48,48,2,48,1]{0,1,2,4,3:T(8,128)} %copy.176, f32[48,2,2,48]{3,0,1,2:T(8,128)S(1)} %get-tuple-element.772), kind=kOutput, calls=%fused_computation.148.clone.1 | convolution fusion | flops 254803968 | bytes 1806336 | tf_op jit(solution)/shard_map/while/body/eval_jaxpr/dot_general | solution.py:79
  91.4 6.0 %fusion.383 = f32[48,48,2,48,1]{0,3,4,2,1:T(8,128)S(1)} fusion(f32[48,48,2,48,1]{0,1,2,4,3:T(8,128)} %copy.177, f32[48,2,2,48]{3,0,1,2:T(8,128)S(1)} %get-tuple-element.772), kind=kOutput, calls=%fused_computation.152.clone.1 | convolution fusion | flops 254803968 | bytes 1806336 | tf_op jit(solution)/shard_map/while/body/eval_jaxpr/dot_general | solution.py:79
  101.0 9.6 %fusion.370 = (f32[48,48,1,48]{3,1,2,0:T(8,128)}, f32[48,48,1,48]{3,1,2,0:T(8,128)}, f32[48,48,1,48]{3,1,2,0:T(8,128)S(1)}, f32[48,48,1,48]{3,1,2,0:T(8,128)S(1)}) fusion(f32[48,48,48]{2,1,0:T(8,128)S(1)} %copy-done.18, f32[48]{0:T(128)S(1)} %get-tuple-element.785, f32[48,48]{1,0:T(8,128)S(1)} %copy-done.24, f32[48,48,2,48]{3,1,2,0:T(8,128)S(1)} %fusion.366, ...), kind=kLoop, calls=%fused_computation.93.clone.1 | loop fusion | flops 1769472 | bytes 3557568 | tf_op jit(solution)/shard_map/while/body/eval_jaxpr/sub | solution.py:110
  118.0 6.0 %fusion.372 = f32[48,48,2,48,1]{0,3,4,2,1:T(8,128)S(1)} fusion(f32[48,48,2,48,1]{0,1,2,4,3:T(8,128)} %copy.172, f32[48,2,2,48]{3,0,1,2:T(8,128)S(1)} %get-tuple-element.772), kind=kOutput, calls=%fused_computation.132.clone.1 | convolution fusion | flops 254803968 | bytes 1806336 | tf_op jit(solution)/shard_map/while/body/eval_jaxpr/dot_general | solution.py:79
  131.0 4.1 copy.173
  135.2 6.0 %fusion.374 = f32[48,48,2,48,1]{0,3,4,2,1:T(8,128)S(1)} fusion(f32[48,48,2,48,1]{0,1,2,4,3:T(8,128)} %copy.173, f32[48,2,2,48]{3,0,1,2:T(8,128)S(1)} %get-tuple-element.772), kind=kOutput, calls=%fused_computation.136.clone.1 | convolution fusion | flops 254803968 | bytes 1806336 | tf_op jit(solution)/shard_map/while/body/eval_jaxpr/dot_general | solution.py:79
  144.8 9.6 %fusion.375 = (f32[48,48,1,48]{3,1,2,0:T(8,128)}, f32[48,48,1,48]{3,1,2,0:T(8,128)}, f32[48,48,1,48]{3,1,2,0:T(8,128)S(1)}, f32[48,48,1,48]{3,1,2,0:T(8,128)S(1)}) fusion(f32[48,48,48]{2,1,0:T(8,128)S(1)} %copy-done.14, f32[48]{0:T(128)S(1)} %get-tuple-element.782, f32[48,48]{1,0:T(8,128)S(1)} %copy-done.26, f32[48,48,2,48]{3,1,2,0:T(8,128)S(1)} %fusion.366, ...), kind=kLoop, calls=%fused_computation.105.clone.1 | loop fusion | flops 1769472 | bytes 3557568 | tf_op jit(solution)/shard_map/while/body/eval_jaxpr/sub | solution.py:110
  159.2 6.0 %fusion.377 = f32[48,48,2,48,1]{0,3,4,2,1:T(8,128)S(1)} fusion(f32[48,48,2,48,1]{0,1,2,4,3:T(8,128)} %copy.174, f32[48,2,2,48]{3,0,1,2:T(8,128)S(1)} %get-tuple-element.772), kind=kOutput, calls=%fused_computation.140.clone.1 | convolution fusion | flops 254803968 | bytes 1806336 | tf_op jit(solution)/shard_map/while/body/eval_jaxpr/dot_general | solution.py:79
  174.7 6.0 %fusion.379 = f32[48,48,2,48,1]{0,3,4,2,1:T(8,128)S(1)} fusion(f32[48,48,2,48,1]{0,1,2,4,3:T(8,128)} %copy.175, f32[48,2,2,48]{3,0,1,2:T(8,128)S(1)} %get-tuple-element.772), kind=kOutput, calls=%fused_computation.144.clone.1 | convolution fusion | flops 254803968 | bytes 1806336 | tf_op jit(solution)/shard_map/while/body/eval_jaxpr/dot_general | solution.py:79
  191.7 6.2 %fusion.369 = f32[48,48,2,48,1]{0,3,4,2,1:T(8,128)S(1)} fusion(f32[48,48,2,48,1]{0,1,2,4,3:T(8,128)} %copy.171, f32[48,2,2,48]{3,0,1,2:T(8,128)S(1)} %get-tuple-element.772), kind=kOutput, calls=%fused_computation.128.clone.1 | convolution fusion | flops 254803968 | bytes 1806336 | tf_op jit(solution)/shard_map/while/body/eval_jaxpr/dot_general | solution.py:79
  200.2 4.2 fusion.384
  220.4 6.0 %fusion.365 = f32[48,48,2,48,1]{0,3,4,2,1:T(8,128)S(1)} fusion(f32[48,48,2,48,1]{1,0,2,4,3:T(8,128)} %copy.170, f32[48,2,2,48]{3,0,1,2:T(8,128)S(1)} %get-tuple-element.770), kind=kOutput, calls=%fused_computation.156.clone.1 | convolution fusion | flops 254803968 | bytes 1806336 | tf_op jit(solution)/shard_map/while/body/eval_jaxpr/dot_general | solution.py:79
  228.6 10.0 %fusion.367 = (f32[48,48,1,48]{3,1,2,0:T(8,128)}, f32[48,48,1,48]{3,1,2,0:T(8,128)}, f32[48,48,1,48]{3,1,2,0:T(8,128)S(1)}, f32[48,48,1,48]{3,1,2,0:T(8,128)S(1)...) fusion(f32[48,48,48]{2,1,0:T(8,128)S(1)} %copy-done.16, f32[48]{0:T(128)S(1)} %get-tuple-element.779, ...), kind=kLoop, calls=%fused_computation.117.clone.1 | loop fusion | flops 2211840 | bytes 4884672 | tf_op jit(solution)/shard_map/while/body/eval_jaxpr/sub | solution.py:110
  246.0 6.0 %fusion.381 = f32[48,48,2,48,1]{0,3,4,2,1:T(8,128)S(1)} fusion(f32[48,48,2,48,1]{0,1,2,4,3:T(8,128)} %copy.176, f32[48,2,2,48]{3,0,1,2:T(8,128)S(1)} %get-tuple-element.772), kind=kOutput, calls=%fused_computation.148.clone.1 | convolution fusion | flops 254803968 | bytes 1806336 | tf_op jit(solution)/shard_map/while/body/eval_jaxpr/dot_general | solution.py:79
  262.9 6.0 %fusion.383 = f32[48,48,2,48,1]{0,3,4,2,1:T(8,128)S(1)} fusion(f32[48,48,2,48,1]{0,1,2,4,3:T(8,128)} %copy.177, f32[48,2,2,48]{3,0,1,2:T(8,128)S(1)} %get-tuple-element.772), kind=kOutput, calls=%fused_computation.152.clone.1 | convolution fusion | flops 254803968 | bytes 1806336 | tf_op jit(solution)/shard_map/while/body/eval_jaxpr/dot_general | solution.py:79
  272.5 9.6 %fusion.370 = (f32[48,48,1,48]{3,1,2,0:T(8,128)}, f32[48,48,1,48]{3,1,2,0:T(8,128)}, f32[48,48,1,48]{3,1,2,0:T(8,128)S(1)}, f32[48,48,1,48]{3,1,2,0:T(8,128)S(1)}) fusion(f32[48,48,48]{2,1,0:T(8,128)S(1)} %copy-done.18, f32[48]{0:T(128)S(1)} %get-tuple-element.785, f32[48,48]{1,0:T(8,128)S(1)} %copy-done.24, f32[48,48,2,48]{3,1,2,0:T(8,128)S(1)} %fusion.366, ...), kind=kLoop, calls=%fused_computation.93.clone.1 | loop fusion | flops 1769472 | bytes 3557568 | tf_op jit(solution)/shard_map/while/body/eval_jaxpr/sub | solution.py:110
  285.5 4.2 %copy.172 = f32[48,48,2,48,1]{0,1,2,4,3:T(8,128)} copy(f32[48,48,2,48,1]{3,1,2,0,4:T(8,128)} %fusion.371) | data formatting | bytes 1769472 | tf_op jit(solution)/shard_map/while/body/eval_jaxpr/dot_general | solution.py:79
  289.8 6.0 %fusion.372 = f32[48,48,2,48,1]{0,3,4,2,1:T(8,128)S(1)} fusion(f32[48,48,2,48,1]{0,1,2,4,3:T(8,128)} %copy.172, f32[48,2,2,48]{3,0,1,2:T(8,128)S(1)} %get-tuple-element.772), kind=kOutput, calls=%fused_computation.132.clone.1 | convolution fusion | flops 254803968 | bytes 1806336 | tf_op jit(solution)/shard_map/while/body/eval_jaxpr/dot_general | solution.py:79
  306.6 6.0 %fusion.374 = f32[48,48,2,48,1]{0,3,4,2,1:T(8,128)S(1)} fusion(f32[48,48,2,48,1]{0,1,2,4,3:T(8,128)} %copy.173, f32[48,2,2,48]{3,0,1,2:T(8,128)S(1)} %get-tuple-element.772), kind=kOutput, calls=%fused_computation.136.clone.1 | convolution fusion | flops 254803968 | bytes 1806336 | tf_op jit(solution)/shard_map/while/body/eval_jaxpr/dot_general | solution.py:79
  316.3 9.6 %fusion.375 = (f32[48,48,1,48]{3,1,2,0:T(8,128)}, f32[48,48,1,48]{3,1,2,0:T(8,128)}, f32[48,48,1,48]{3,1,2,0:T(8,128)S(1)}, f32[48,48,1,48]{3,1,2,0:T(8,128)S(1)}) fusion(f32[48,48,48]{2,1,0:T(8,128)S(1)} %copy-done.14, f32[48]{0:T(128)S(1)} %get-tuple-element.782, f32[48,48]{1,0:T(8,128)S(1)} %copy-done.26, f32[48,48,2,48]{3,1,2,0:T(8,128)S(1)} %fusion.366, ...), kind=kLoop, calls=%fused_computation.105.clone.1 | loop fusion | flops 1769472 | bytes 3557568 | tf_op jit(solution)/shard_map/while/body/eval_jaxpr/sub | solution.py:110
  330.7 6.0 %fusion.377 = f32[48,48,2,48,1]{0,3,4,2,1:T(8,128)S(1)} fusion(f32[48,48,2,48,1]{0,1,2,4,3:T(8,128)} %copy.174, f32[48,2,2,48]{3,0,1,2:T(8,128)S(1)} %get-tuple-element.772), kind=kOutput, calls=%fused_computation.140.clone.1 | convolution fusion | flops 254803968 | bytes 1806336 | tf_op jit(solution)/shard_map/while/body/eval_jaxpr/dot_general | solution.py:79
  346.3 6.0 %fusion.379 = f32[48,48,2,48,1]{0,3,4,2,1:T(8,128)S(1)} fusion(f32[48,48,2,48,1]{0,1,2,4,3:T(8,128)} %copy.175, f32[48,2,2,48]{3,0,1,2:T(8,128)S(1)} %get-tuple-element.772), kind=kOutput, calls=%fused_computation.144.clone.1 | convolution fusion | flops 254803968 | bytes 1806336 | tf_op jit(solution)/shard_map/while/body/eval_jaxpr/dot_general | solution.py:79
  363.3 6.2 %fusion.369 = f32[48,48,2,48,1]{0,3,4,2,1:T(8,128)S(1)} fusion(f32[48,48,2,48,1]{0,1,2,4,3:T(8,128)} %copy.171, f32[48,2,2,48]{3,0,1,2:T(8,128)S(1)} %get-tuple-element.772), kind=kOutput, calls=%fused_computation.128.clone.1 | convolution fusion | flops 254803968 | bytes 1806336 | tf_op jit(solution)/shard_map/while/body/eval_jaxpr/dot_general | solution.py:79
  371.8 4.2 fusion.384
  386.5 4.4 %all-to-all-start.1 = ((f32[2,48,2304]{2,0,1:T(2,128)}), f32[2,48,2304]{2,0,1:T(2,128)}, u32[]{:S(2)}, u32[]{:S(2)}) async-start(f32[2,48,2304]{2,0,1:T(2,128)} %get-tuple-element.142), calls=%async_computation.1 | async-start | bytes 1769472 | tf_op jit(solution)/shard_map/all_to_all | solution.py:139
  402.2 10.9 %all-to-all-done.1 = f32[2,48,2304]{2,0,1:T(2,128)} async-done(((f32[2,48,2304]{2,0,1:T(2,128)}), f32[2,48,2304]{2,0,1:T(2,128)}, u32[]{:S(2)}, u32[]{:S(2)}) %all-to-all-start.1) | async-done | bytes 884768 | tf_op jit(solution)/shard_map/all_to_all | solution.py:139
  (206 shorter events, 190.8 us)
Async XLA Ops:
  2.8 35.8 %all-to-all-start = ((f32[16,6,2304]{2,1,0:T(8,128)}), f32[16,6,2304]{2,1,0:T(8,128)S(1)}, u32[]{:S(2)}, u32[]{:S(2)}) async-start(f32[16,6,2304]{2,1,0:T(8,128)} %copy.77), calls=%async_computation | async-start | bytes 2359296 | tf_op jit(solution)/shard_map/all_to_all | solution.py:137
  10.0 14.1 %copy-start.31 = (f32[48]{0:T(128)}, f32[48]{0:T(128)S(1)}, u32[]{:S(2)}) copy-start(f32[48]{0:T(128)S(1)} %get-tuple-element.734) | copy-start | bytes 580
  10.6 13.6 %copy-start.21 = (f32[48,48]{1,0:T(8,128)}, f32[48,48]{1,0:T(8,128)S(1)}, u32[]{:S(2)}) copy-start(f32[48,48]{1,0:T(8,128)S(1)} %get-tuple-element.736) | copy-start | bytes 27652
  10.6 13.6 %copy-start.23 = (f32[48,48]{1,0:T(8,128)}, f32[48,48]{1,0:T(8,128)S(1)}, u32[]{:S(2)}) copy-start(f32[48,48]{1,0:T(8,128)S(1)} %get-tuple-element.738) | copy-start | bytes 27652
  10.6 13.6 %copy-start.25 = (f32[48,48]{1,0:T(8,128)}, f32[48,48]{1,0:T(8,128)S(1)}, u32[]{:S(2)}) copy-start(f32[48,48]{1,0:T(8,128)S(1)} %get-tuple-element.735) | copy-start | bytes 27652
  10.6 13.6 %copy-start.27 = (f32[48,48]{1,0:T(8,128)}, f32[48,48]{1,0:T(8,128)S(1)}, u32[]{:S(2)}) copy-start(f32[48,48]{1,0:T(8,128)S(1)} %get-tuple-element.732) | copy-start | bytes 27652
  80.5 3.5 copy-start.6
  80.5 3.5 copy-start.7
  97.4 3.6 copy-start.17
  97.4 3.5 copy-start.18
  97.4 3.5 copy-start.24
  141.2 3.6 copy-start.13
  141.2 3.6 copy-start.14
  141.2 3.6 copy-start.22
  141.2 3.6 copy-start.26
  191.7 8.3 %copy-start.2 = (f32[48,48,2,48]{3,1,2,0:T(8,128)S(1)}, f32[48,48,2,48]{3,1,2,0:T(8,128)}, u32[]{:S(2)}) copy-start(f32[48,48,2,48]{3,1,2,0:T(8,128)} %bitcast_multiply_fusion.41) | copy-start | bytes 2654212 | tf_op jit(solution)/shard_map/while
  191.7 8.3 %copy-start.3 = (f32[48,48,2,48]{3,1,2,0:T(8,128)S(1)}, f32[48,48,2,48]{3,1,2,0:T(8,128)}, u32[]{:S(2)}) copy-start(f32[48,48,2,48]{3,1,2,0:T(8,128)} %bitcast_multiply_fusion.42) | copy-start | bytes 2654212 | tf_op jit(solution)/shard_map/while
  252.0 3.5 copy-start.6
  268.9 3.6 copy-start.17
  269.0 3.5 copy-start.18
  269.0 3.5 copy-start.24
  312.7 3.6 copy-start.13
  312.7 3.6 copy-start.14
  312.7 3.6 copy-start.22
  312.7 3.6 copy-start.26
  363.3 8.3 %copy-start.2 = (f32[48,48,2,48]{3,1,2,0:T(8,128)S(1)}, f32[48,48,2,48]{3,1,2,0:T(8,128)}, u32[]{:S(2)}) copy-start(f32[48,48,2,48]{3,1,2,0:T(8,128)} %bitcast_multiply_fusion.41) | copy-start | bytes 2654212 | tf_op jit(solution)/shard_map/while
  363.3 8.3 %copy-start.3 = (f32[48,48,2,48]{3,1,2,0:T(8,128)S(1)}, f32[48,48,2,48]{3,1,2,0:T(8,128)}, u32[]{:S(2)}) copy-start(f32[48,48,2,48]{3,1,2,0:T(8,128)} %bitcast_multiply_fusion.42) | copy-start | bytes 2654212 | tf_op jit(solution)/shard_map/while
  386.5 4.4 %copy-start.19 = (f32[16,6,2304]{2,0,1:T(8,128)S(1)}, f32[16,6,2304]{2,0,1:T(8,128)}, u32[]{:S(2)}) copy-start(f32[16,6,2304]{2,0,1:T(8,128)} %param.6) | copy-start | bytes 2654212
  386.5 7.1 %copy-start.34 = (s32[64]{0:T(128)S(1)}, s32[64]{0:T(128)}, u32[]{:S(2)}) copy-start(s32[64]{0:T(128)} %param.8) | copy-start | bytes 772
  386.5 26.5 %all-to-all-start.1 = ((f32[2,48,2304]{2,0,1:T(2,128)}), f32[2,48,2304]{2,0,1:T(2,128)}, u32[]{:S(2)}, u32[]{:S(2)}) async-start(f32[2,48,2304]{2,0,1:T(2,128)} %get-tuple-element.142), calls=%async_computation.1 | async-start | bytes 1769472 | tf_op jit(solution)/shard_map/all_to_all | solution.py:139
  391.0 26.1 %collective-permute-start = (f32[1,6,2304]{2,0,1:T(1,128)S(1)}, f32[1,6,2304]{2,0,1:T(1,128)S(1)}, u32[]{:S(2)}, u32[]{:S(2)}) collective-permute-start(f32[1,6,2304]{2,0,1:T(1,128)S(1)} %get-tuple-element.523), channel_id=1, source_target_pairs={{0,8},{8,16},{16,24},{1,9},{9,17},{17,25},{2,10},{10,18},{18,26},{... | collective-permute-start | bytes 165896 | tf_op jit(solution)/shard_map/ppermute | solution.py:31
  392.3 24.9 %collective-permute-start.1 = (f32[1,6,2304]{2,0,1:T(1,128)S(1)}, f32[1,6,2304]{2,0,1:T(1,128)S(1)}, u32[]{:S(2)}, u32[]{:S(2)}) collective-permute-start(f32[1,6,2304]{2,0,1:T(1,128)S(1)} %get-tuple-element.524), channel_id=1, source_target_pairs={{8,0},{16,8},{24,16},{9,1},{17,9},{25,17},{10,2},{18,10},{26,18},{... | collective-permute-start | bytes 165896 | tf_op jit(solution)/shard_map/ppermute | solution.py:33
  (32 other events, 76.8 us)
where the time goes:
time: 423 us; the launch traced here: 419 us
  matrix products  196 us (46%)
  local copies, waits for them, and re-layouts  94.4 us (22%)
  other arithmetic  82.4 us (19%)
  waiting for transfers between devices  25.3 us (6%)
  starting transfers between devices  14.2 us (3%)
  loops' own time  5.61 us (1%)
    dot_general x48, matrix products, apply_table(): lax.dot_general(tensor, table, ((dims, tuple(range(len(dims)))), ((), ())...  196 us
    dot_general x16, local copies, waits for them, and re-layouts, apply_table(): lax.dot_general(tensor, table, ((dims, tuple(range(len(dims)))), ((), ())...  60.6 us
    sub x6, other arithmetic, packed(): joined_real = first_factor * real_part - second_factor * imag_part  58.4 us
    all_to_all x1, waiting for transfers between devices, body(): lax.all_to_all(distribution, 'vel', split_axis=0, concat_axis=1, tiled=True)  14.4 us
    div x1, other arithmetic, kernel_tables(): loss_total = sum(loss_tables) / 6.0  13.5 us
    all_to_all x1, waiting for transfers between devices, body(): lax.all_to_all(cell_terms, 'vel', split_axis=1, concat_axis=0, tiled=True)  10.9 us
  transfers between devices with their start and end apart: 4, of which 2 were waited for; matrix products, arithmetic and copies ran while one was open for 6% of the time, Pallas kernels for 0%

commit v1 on v0

--- a/solution.py
+++ b/solution.py
@@ -136,7 +136,10 @@
 
     regrouped = lax.all_to_all(distribution, "vel", split_axis=0, concat_axis=1, tiled=True)
     cell_terms = lax.map(from_cell, regrouped)
-    collision_term = lax.all_to_all(cell_terms, "vel", split_axis=1, concat_axis=0, tiled=True)
+    size = lax.axis_size("vel")
+    pieces = jnp.stack(jnp.split(cell_terms, size, axis=1), axis=0)
+    pieces = lax.all_to_all(pieces, "vel", split_axis=0, concat_axis=0)
+    collision_term = jnp.concatenate(pieces, axis=0)
     offset = lax.axis_index("space") * cell_count
     padded = padded_2(distribution, (("space", 0),), 1)
     mirror = distribution.reshape(cell_count, planes_dev, points, points)[:, :, ::-1, :].reshape(

time: 423 us -> 435 us (1.028)
  local copies, waits for them, and re-layouts: 94.4 us -> 107 us
    unnamed x22 -> x29, local copies, waits for them, and re-layouts: 3.04 us -> 14 us
where the time goes in v1:
time: 435 us; the launch traced here: 431 us
  matrix products  196 us (45%)
  local copies, waits for them, and re-layouts  107 us (25%)
  other arithmetic  82.4 us (19%)
  waiting for transfers between devices  25.3 us (6%)
  starting transfers between devices  14.1 us (3%)
  loops' own time  5.72 us (1%)
    dot_general x48, matrix products, apply_table(): lax.dot_general(tensor, table, ((dims, tuple(range(len(dims)))), ((), ())...  196 us
    dot_general x16, local copies, waits for them, and re-layouts, apply_table(): lax.dot_general(tensor, table, ((dims, tuple(range(len(dims)))), ((), ())...  60.6 us
    sub x6, other arithmetic, packed(): joined_real = first_factor * real_part - second_factor * imag_part  58.4 us
    all_to_all x1, waiting for transfers between devices, body(): lax.all_to_all(distribution, 'vel', split_axis=0, concat_axis=1, tiled=True)  14.4 us
    unnamed x29, local copies, waits for them, and re-layouts  14 us
    div x1, other arithmetic, kernel_tables(): loss_total = sum(loss_tables) / 6.0  13.5 us
    all_to_all x1, waiting for transfers between devices, body(): pieces = lax.all_to_all(pieces, 'vel', split_axis=0, concat_axis=0)  10.9 us
  transfers between devices with their start and end apart: 4, of which 2 were waited for; matrix products, arithmetic and copies ran while one was open for 6% of the time, Pallas kernels for 0%

profile of v1, /device:TPU:0, one launch (start us, length us, event | category | flops | bytes accessed | tf_op | source)
XLA Modules:
  0.0 431.1 jit_solution(18243857552264541438)
XLA Ops:
  2.8 7.3 %all-to-all-start = ((f32[16,6,2304]{2,1,0:T(8,128)}), f32[16,6,2304]{2,1,0:T(8,128)S(1)}, u32[]{:S(2)}, u32[]{:S(2)}) async-start(f32[16,6,2304]{2,1,0:T(8,128)} %copy.61), calls=%async_computation | async-start | bytes 2359296 | tf_op jit(solution)/shard_map/all_to_all | solution.py:137
  10.6 13.5 %add_multiply_fusion = (f32[48,48,48]{2,1,0:T(8,128)}, f32[48,48,48]{2,1,0:T(8,128)}, f32[48,48,48]{2,1,0:T(8,128)}, f32[48,48,48]{2,1,0:T(8,128)}, f32[48,48,48...) fusion(f32[48]{0:T(128)S(1)} %get-tuple-element.715, f32[48,48]{1,0:T(8,128)S(1)} %get-tuple-element.717, ...), kind=kLoop, calls=%fused_computation.329 | loop fusion | flops 26652672 | bytes 3161856 | tf_op jit(solution)/shard_map/div | solution.py:58
  24.2 14.4 %all-to-all-done = f32[16,6,2304]{2,1,0:T(8,128)S(1)} async-done(((f32[16,6,2304]{2,1,0:T(8,128)}), f32[16,6,2304]{2,1,0:T(8,128)S(1)}, u32[]{:S(2)}, u32[]{:S(2)}) %all-to-all-start) | async-done | bytes 884768 | tf_op jit(solution)/shard_map/all_to_all | solution.py:137
  39.3 347.1 %while.13 = (s32[]{:T(128)}, f32[2,48,2304]{2,0,1:T(2,128)}, f32[2,48,2304]{2,0,1:T(2,128)S(1)}, f32[48,2,48]{2,0,1:T(8,128)S(1)}, f32[48,2,2,48]{3,0,1,2:T(8,12...) while((s32[]{:T(128)}, f32[2,48,2304]{2,0,1:T(2,128)}, ...), condition=%wide.region_1.3_spmd.clone.clone.clone, body=%wide.region_0.2_spmd.clone.clone.clone.sunk | while | flops 5998288896 | bytes 128030208 | solution.py:138
  49.0 6.0 %fusion.365 = f32[48,48,2,48,1]{0,3,4,2,1:T(8,128)S(1)} fusion(f32[48,48,2,48,1]{1,0,2,4,3:T(8,128)} %copy.161, f32[48,2,2,48]{3,0,1,2:T(8,128)S(1)} %get-tuple-element.748), kind=kOutput, calls=%fused_computation.156.clone.1 | convolution fusion | flops 254803968 | bytes 1806336 | tf_op jit(solution)/shard_map/while/body/eval_jaxpr/dot_general | solution.py:79
  57.1 10.0 %fusion.367 = (f32[48,48,1,48]{3,1,2,0:T(8,128)}, f32[48,48,1,48]{3,1,2,0:T(8,128)}, f32[48,48,1,48]{3,1,2,0:T(8,128)S(1)}, f32[48,48,1,48]{3,1,2,0:T(8,128)S(1)...) fusion(f32[48,48,48]{2,1,0:T(8,128)S(1)} %copy-done.16, f32[48]{0:T(128)S(1)} %get-tuple-element.757, ...), kind=kLoop, calls=%fused_computation.117.clone.1 | loop fusion | flops 2211840 | bytes 4884672 | tf_op jit(solution)/shard_map/while/body/eval_jaxpr/sub | solution.py:110
  74.5 6.0 %fusion.381 = f32[48,48,2,48,1]{0,3,4,2,1:T(8,128)S(1)} fusion(f32[48,48,2,48,1]{0,1,2,4,3:T(8,128)} %copy.167, f32[48,2,2,48]{3,0,1,2:T(8,128)S(1)} %get-tuple-element.750), kind=kOutput, calls=%fused_computation.148.clone.1 | convolution fusion | flops 254803968 | bytes 1806336 | tf_op jit(solution)/shard_map/while/body/eval_jaxpr/dot_general | solution.py:79
  91.4 6.0 %fusion.383 = f32[48,48,2,48,1]{0,3,4,2,1:T(8,128)S(1)} fusion(f32[48,48,2,48,1]{0,1,2,4,3:T(8,128)} %copy.168, f32[48,2,2,48]{3,0,1,2:T(8,128)S(1)} %get-tuple-element.750), kind=kOutput, calls=%fused_computation.152.clone.1 | convolution fusion | flops 254803968 | bytes 1806336 | tf_op jit(solution)/shard_map/while/body/eval_jaxpr/dot_general | solution.py:79
  101.0 9.6 %fusion.370 = (f32[48,48,1,48]{3,1,2,0:T(8,128)}, f32[48,48,1,48]{3,1,2,0:T(8,128)}, f32[48,48,1,48]{3,1,2,0:T(8,128)S(1)}, f32[48,48,1,48]{3,1,2,0:T(8,128)S(1)}) fusion(f32[48,48,48]{2,1,0:T(8,128)S(1)} %copy-done.18, f32[48]{0:T(128)S(1)} %get-tuple-element.763, f32[48,48]{1,0:T(8,128)S(1)} %copy-done.24, f32[48,48,2,48]{3,1,2,0:T(8,128)S(1)} %fusion.366, ...), kind=kLoop, calls=%fused_computation.93.clone.1 | loop fusion | flops 1769472 | bytes 3557568 | tf_op jit(solution)/shard_map/while/body/eval_jaxpr/sub | solution.py:110
  118.0 6.0 %fusion.372 = f32[48,48,2,48,1]{0,3,4,2,1:T(8,128)S(1)} fusion(f32[48,48,2,48,1]{0,1,2,4,3:T(8,128)} %copy.163, f32[48,2,2,48]{3,0,1,2:T(8,128)S(1)} %get-tuple-element.750), kind=kOutput, calls=%fused_computation.132.clone.1 | convolution fusion | flops 254803968 | bytes 1806336 | tf_op jit(solution)/shard_map/while/body/eval_jaxpr/dot_general | solution.py:79
  131.0 4.1 copy.164
  135.2 6.0 %fusion.374 = f32[48,48,2,48,1]{0,3,4,2,1:T(8,128)S(1)} fusion(f32[48,48,2,48,1]{0,1,2,4,3:T(8,128)} %copy.164, f32[48,2,2,48]{3,0,1,2:T(8,128)S(1)} %get-tuple-element.750), kind=kOutput, calls=%fused_computation.136.clone.1 | convolution fusion | flops 254803968 | bytes 1806336 | tf_op jit(solution)/shard_map/while/body/eval_jaxpr/dot_general | solution.py:79
  144.8 9.6 %fusion.375 = (f32[48,48,1,48]{3,1,2,0:T(8,128)}, f32[48,48,1,48]{3,1,2,0:T(8,128)}, f32[48,48,1,48]{3,1,2,0:T(8,128)S(1)}, f32[48,48,1,48]{3,1,2,0:T(8,128)S(1)}) fusion(f32[48,48,48]{2,1,0:T(8,128)S(1)} %copy-done.14, f32[48]{0:T(128)S(1)} %get-tuple-element.760, f32[48,48]{1,0:T(8,128)S(1)} %copy-done.26, f32[48,48,2,48]{3,1,2,0:T(8,128)S(1)} %fusion.366, ...), kind=kLoop, calls=%fused_computation.105.clone.1 | loop fusion | flops 1769472 | bytes 3557568 | tf_op jit(solution)/shard_map/while/body/eval_jaxpr/sub | solution.py:110
  159.2 6.0 %fusion.377 = f32[48,48,2,48,1]{0,3,4,2,1:T(8,128)S(1)} fusion(f32[48,48,2,48,1]{0,1,2,4,3:T(8,128)} %copy.165, f32[48,2,2,48]{3,0,1,2:T(8,128)S(1)} %get-tuple-element.750), kind=kOutput, calls=%fused_computation.140.clone.1 | convolution fusion | flops 254803968 | bytes 1806336 | tf_op jit(solution)/shard_map/while/body/eval_jaxpr/dot_general | solution.py:79
  174.7 6.0 %fusion.379 = f32[48,48,2,48,1]{0,3,4,2,1:T(8,128)S(1)} fusion(f32[48,48,2,48,1]{0,1,2,4,3:T(8,128)} %copy.166, f32[48,2,2,48]{3,0,1,2:T(8,128)S(1)} %get-tuple-element.750), kind=kOutput, calls=%fused_computation.144.clone.1 | convolution fusion | flops 254803968 | bytes 1806336 | tf_op jit(solution)/shard_map/while/body/eval_jaxpr/dot_general | solution.py:79
  191.7 6.2 %fusion.369 = f32[48,48,2,48,1]{0,3,4,2,1:T(8,128)S(1)} fusion(f32[48,48,2,48,1]{0,1,2,4,3:T(8,128)} %copy.162, f32[48,2,2,48]{3,0,1,2:T(8,128)S(1)} %get-tuple-element.750), kind=kOutput, calls=%fused_computation.128.clone.1 | convolution fusion | flops 254803968 | bytes 1806336 | tf_op jit(solution)/shard_map/while/body/eval_jaxpr/dot_general | solution.py:79
  200.2 4.2 fusion.384
  220.3 6.0 %fusion.365 = f32[48,48,2,48,1]{0,3,4,2,1:T(8,128)S(1)} fusion(f32[48,48,2,48,1]{1,0,2,4,3:T(8,128)} %copy.161, f32[48,2,2,48]{3,0,1,2:T(8,128)S(1)} %get-tuple-element.748), kind=kOutput, calls=%fused_computation.156.clone.1 | convolution fusion | flops 254803968 | bytes 1806336 | tf_op jit(solution)/shard_map/while/body/eval_jaxpr/dot_general | solution.py:79
  228.5 10.0 %fusion.367 = (f32[48,48,1,48]{3,1,2,0:T(8,128)}, f32[48,48,1,48]{3,1,2,0:T(8,128)}, f32[48,48,1,48]{3,1,2,0:T(8,128)S(1)}, f32[48,48,1,48]{3,1,2,0:T(8,128)S(1)...) fusion(f32[48,48,48]{2,1,0:T(8,128)S(1)} %copy-done.16, f32[48]{0:T(128)S(1)} %get-tuple-element.757, ...), kind=kLoop, calls=%fused_computation.117.clone.1 | loop fusion | flops 2211840 | bytes 4884672 | tf_op jit(solution)/shard_map/while/body/eval_jaxpr/sub | solution.py:110
  245.9 6.0 %fusion.381 = f32[48,48,2,48,1]{0,3,4,2,1:T(8,128)S(1)} fusion(f32[48,48,2,48,1]{0,1,2,4,3:T(8,128)} %copy.167, f32[48,2,2,48]{3,0,1,2:T(8,128)S(1)} %get-tuple-element.750), kind=kOutput, calls=%fused_computation.148.clone.1 | convolution fusion | flops 254803968 | bytes 1806336 | tf_op jit(solution)/shard_map/while/body/eval_jaxpr/dot_general | solution.py:79
  262.8 6.0 %fusion.383 = f32[48,48,2,48,1]{0,3,4,2,1:T(8,128)S(1)} fusion(f32[48,48,2,48,1]{0,1,2,4,3:T(8,128)} %copy.168, f32[48,2,2,48]{3,0,1,2:T(8,128)S(1)} %get-tuple-element.750), kind=kOutput, calls=%fused_computation.152.clone.1 | convolution fusion | flops 254803968 | bytes 1806336 | tf_op jit(solution)/shard_map/while/body/eval_jaxpr/dot_general | solution.py:79
  272.4 9.6 %fusion.370 = (f32[48,48,1,48]{3,1,2,0:T(8,128)}, f32[48,48,1,48]{3,1,2,0:T(8,128)}, f32[48,48,1,48]{3,1,2,0:T(8,128)S(1)}, f32[48,48,1,48]{3,1,2,0:T(8,128)S(1)}) fusion(f32[48,48,48]{2,1,0:T(8,128)S(1)} %copy-done.18, f32[48]{0:T(128)S(1)} %get-tuple-element.763, f32[48,48]{1,0:T(8,128)S(1)} %copy-done.24, f32[48,48,2,48]{3,1,2,0:T(8,128)S(1)} %fusion.366, ...), kind=kLoop, calls=%fused_computation.93.clone.1 | loop fusion | flops 1769472 | bytes 3557568 | tf_op jit(solution)/shard_map/while/body/eval_jaxpr/sub | solution.py:110
  285.5 4.2 copy.163
  289.7 6.0 %fusion.372 = f32[48,48,2,48,1]{0,3,4,2,1:T(8,128)S(1)} fusion(f32[48,48,2,48,1]{0,1,2,4,3:T(8,128)} %copy.163, f32[48,2,2,48]{3,0,1,2:T(8,128)S(1)} %get-tuple-element.750), kind=kOutput, calls=%fused_computation.132.clone.1 | convolution fusion | flops 254803968 | bytes 1806336 | tf_op jit(solution)/shard_map/while/body/eval_jaxpr/dot_general | solution.py:79
  306.6 6.0 %fusion.374 = f32[48,48,2,48,1]{0,3,4,2,1:T(8,128)S(1)} fusion(f32[48,48,2,48,1]{0,1,2,4,3:T(8,128)} %copy.164, f32[48,2,2,48]{3,0,1,2:T(8,128)S(1)} %get-tuple-element.750), kind=kOutput, calls=%fused_computation.136.clone.1 | convolution fusion | flops 254803968 | bytes 1806336 | tf_op jit(solution)/shard_map/while/body/eval_jaxpr/dot_general | solution.py:79
  316.2 9.6 %fusion.375 = (f32[48,48,1,48]{3,1,2,0:T(8,128)}, f32[48,48,1,48]{3,1,2,0:T(8,128)}, f32[48,48,1,48]{3,1,2,0:T(8,128)S(1)}, f32[48,48,1,48]{3,1,2,0:T(8,128)S(1)}) fusion(f32[48,48,48]{2,1,0:T(8,128)S(1)} %copy-done.14, f32[48]{0:T(128)S(1)} %get-tuple-element.760, f32[48,48]{1,0:T(8,128)S(1)} %copy-done.26, f32[48,48,2,48]{3,1,2,0:T(8,128)S(1)} %fusion.366, ...), kind=kLoop, calls=%fused_computation.105.clone.1 | loop fusion | flops 1769472 | bytes 3557568 | tf_op jit(solution)/shard_map/while/body/eval_jaxpr/sub | solution.py:110
  330.6 6.0 %fusion.377 = f32[48,48,2,48,1]{0,3,4,2,1:T(8,128)S(1)} fusion(f32[48,48,2,48,1]{0,1,2,4,3:T(8,128)} %copy.165, f32[48,2,2,48]{3,0,1,2:T(8,128)S(1)} %get-tuple-element.750), kind=kOutput, calls=%fused_computation.140.clone.1 | convolution fusion | flops 254803968 | bytes 1806336 | tf_op jit(solution)/shard_map/while/body/eval_jaxpr/dot_general | solution.py:79
  346.2 6.0 %fusion.379 = f32[48,48,2,48,1]{0,3,4,2,1:T(8,128)S(1)} fusion(f32[48,48,2,48,1]{0,1,2,4,3:T(8,128)} %copy.166, f32[48,2,2,48]{3,0,1,2:T(8,128)S(1)} %get-tuple-element.750), kind=kOutput, calls=%fused_computation.144.clone.1 | convolution fusion | flops 254803968 | bytes 1806336 | tf_op jit(solution)/shard_map/while/body/eval_jaxpr/dot_general | solution.py:79
  363.2 6.2 %fusion.369 = f32[48,48,2,48,1]{0,3,4,2,1:T(8,128)S(1)} fusion(f32[48,48,2,48,1]{0,1,2,4,3:T(8,128)} %copy.162, f32[48,2,2,48]{3,0,1,2:T(8,128)S(1)} %get-tuple-element.750), kind=kOutput, calls=%fused_computation.128.clone.1 | convolution fusion | flops 254803968 | bytes 1806336 | tf_op jit(solution)/shard_map/while/body/eval_jaxpr/dot_general | solution.py:79
  371.7 4.2 fusion.384
  398.9 4.2 all-to-all-start.1
  414.4 10.9 %all-to-all-done.1 = f32[8,2,6,2304]{3,1,2,0:T(2,128)} async-done(((f32[8,2,6,2304]{3,1,2,0:T(2,128)}), f32[8,2,6,2304]{3,1,2,0:T(2,128)}, u32[]{:S(2)}, u32[]{:S(2)}) %all-to-all-start.1) | async-done | bytes 884768 | tf_op jit(solution)/shard_map/all_to_all | solution.py:141
  (214 shorter events, 203.1 us)
Async XLA Ops:
  2.8 35.8 %all-to-all-start = ((f32[16,6,2304]{2,1,0:T(8,128)}), f32[16,6,2304]{2,1,0:T(8,128)S(1)}, u32[]{:S(2)}, u32[]{:S(2)}) async-start(f32[16,6,2304]{2,1,0:T(8,128)} %copy.61), calls=%async_computation | async-start | bytes 2359296 | tf_op jit(solution)/shard_map/all_to_all | solution.py:137
  10.0 14.1 %copy-start.31 = (f32[48]{0:T(128)}, f32[48]{0:T(128)S(1)}, u32[]{:S(2)}) copy-start(f32[48]{0:T(128)S(1)} %get-tuple-element.712) | copy-start | bytes 580
  10.6 13.6 %copy-start.21 = (f32[48,48]{1,0:T(8,128)}, f32[48,48]{1,0:T(8,128)S(1)}, u32[]{:S(2)}) copy-start(f32[48,48]{1,0:T(8,128)S(1)} %get-tuple-element.714) | copy-start | bytes 27652
  10.6 13.6 %copy-start.23 = (f32[48,48]{1,0:T(8,128)}, f32[48,48]{1,0:T(8,128)S(1)}, u32[]{:S(2)}) copy-start(f32[48,48]{1,0:T(8,128)S(1)} %get-tuple-element.716) | copy-start | bytes 27652
  10.6 13.6 %copy-start.25 = (f32[48,48]{1,0:T(8,128)}, f32[48,48]{1,0:T(8,128)S(1)}, u32[]{:S(2)}) copy-start(f32[48,48]{1,0:T(8,128)S(1)} %get-tuple-element.713) | copy-start | bytes 27652
  10.6 13.6 %copy-start.27 = (f32[48,48]{1,0:T(8,128)}, f32[48,48]{1,0:T(8,128)S(1)}, u32[]{:S(2)}) copy-start(f32[48,48]{1,0:T(8,128)S(1)} %get-tuple-element.710) | copy-start | bytes 27652
  80.5 3.5 copy-start.6
  97.4 3.6 copy-start.17
  97.4 3.5 copy-start.18
  97.4 3.5 copy-start.24
  141.2 3.6 copy-start.13
  141.2 3.6 copy-start.14
  141.2 3.6 copy-start.22
  141.2 3.6 copy-start.26
  191.7 8.3 %copy-start.2 = (f32[48,48,2,48]{3,1,2,0:T(8,128)S(1)}, f32[48,48,2,48]{3,1,2,0:T(8,128)}, u32[]{:S(2)}) copy-start(f32[48,48,2,48]{3,1,2,0:T(8,128)} %bitcast_multiply_fusion.41) | copy-start | bytes 2654212 | tf_op jit(solution)/shard_map/while
  191.7 8.3 %copy-start.3 = (f32[48,48,2,48]{3,1,2,0:T(8,128)S(1)}, f32[48,48,2,48]{3,1,2,0:T(8,128)}, u32[]{:S(2)}) copy-start(f32[48,48,2,48]{3,1,2,0:T(8,128)} %bitcast_multiply_fusion.42) | copy-start | bytes 2654212 | tf_op jit(solution)/shard_map/while
  251.9 3.5 copy-start.6
  251.9 3.5 copy-start.7
  268.9 3.6 copy-start.17
  268.9 3.5 copy-start.18
  268.9 3.5 copy-start.24
  312.6 3.6 copy-start.13
  312.6 3.6 copy-start.14
  312.6 3.6 copy-start.22
  312.6 3.6 copy-start.26
  363.2 8.3 %copy-start.2 = (f32[48,48,2,48]{3,1,2,0:T(8,128)S(1)}, f32[48,48,2,48]{3,1,2,0:T(8,128)}, u32[]{:S(2)}) copy-start(f32[48,48,2,48]{3,1,2,0:T(8,128)} %bitcast_multiply_fusion.41) | copy-start | bytes 2654212 | tf_op jit(solution)/shard_map/while
  363.2 8.3 %copy-start.3 = (f32[48,48,2,48]{3,1,2,0:T(8,128)S(1)}, f32[48,48,2,48]{3,1,2,0:T(8,128)}, u32[]{:S(2)}) copy-start(f32[48,48,2,48]{3,1,2,0:T(8,128)} %bitcast_multiply_fusion.42) | copy-start | bytes 2654212 | tf_op jit(solution)/shard_map/while
  394.2 9.0 %copy-start.19 = (f32[16,6,2304]{2,0,1:T(8,128)S(1)}, f32[16,6,2304]{2,0,1:T(8,128)}, u32[]{:S(2)}) copy-start(f32[16,6,2304]{2,0,1:T(8,128)} %param.6) | copy-start | bytes 2654212
  395.8 10.0 %copy-start.34 = (s32[64]{0:T(128)S(1)}, s32[64]{0:T(128)}, u32[]{:S(2)}) copy-start(s32[64]{0:T(128)} %param.8) | copy-start | bytes 772
  398.9 26.4 %all-to-all-start.1 = ((f32[8,2,6,2304]{3,1,2,0:T(2,128)}), f32[8,2,6,2304]{3,1,2,0:T(2,128)}, u32[]{:S(2)}, u32[]{:S(2)}) async-start(f32[8,2,6,2304]{3,1,2,0:T(2,128)} %bitcast_dynamic-update-slice_fusion), calls=%async_computation.1 | async-start | bytes 1769472 | tf_op jit(solution)/shard_map/all_to_all | solution.py:141
  403.3 26.1 %collective-permute-start = (f32[1,6,2304]{2,0,1:T(1,128)S(1)}, f32[1,6,2304]{2,0,1:T(1,128)S(1)}, u32[]{:S(2)}, u32[]{:S(2)}) collective-permute-start(f32[1,6,2304]{2,0,1:T(1,128)S(1)} %get-tuple-element.501), channel_id=1, source_target_pairs={{0,8},{8,16},{16,24},{1,9},{9,17},{17,25},{2,10},{10,18},{18,26},{... | collective-permute-start | bytes 165896 | tf_op jit(solution)/shard_map/ppermute | solution.py:31
  404.6 24.9 %collective-permute-start.1 = (f32[1,6,2304]{2,0,1:T(1,128)S(1)}, f32[1,6,2304]{2,0,1:T(1,128)S(1)}, u32[]{:S(2)}, u32[]{:S(2)}) collective-permute-start(f32[1,6,2304]{2,0,1:T(1,128)S(1)} %get-tuple-element.502), channel_id=1, source_target_pairs={{8,0},{16,8},{24,16},{9,1},{17,9},{25,17},{10,2},{18,10},{26,18},{... | collective-permute-start | bytes 165896 | tf_op jit(solution)/shard_map/ppermute | solution.py:33
  (32 other events, 76.6 us)
